TPU v7x, 128 devices: a whole 4x4x4 slice. The times are simulated.
128 devices in a mesh: req: 16 (over y, x), seq: 4 (over z), hid: 2 (over core).
Axes of the slice: x: 4, y: 4, z: 4, core: 2. Of those that a mesh axis runs over, the one named last changes fastest.
Arguments:
- tokens: bfloat16 [65536, 2048], P(('req', 'seq')), may hold values from -6 to 6
- attention_gain: bfloat16 [2048], replicated, may hold values from 0.099609375 to 1.8984375
- project_weight: bfloat16 [2048, 2048], P(None, 'hid'), may hold values from -0.125 to 0.125
- conv_weight: bfloat16 [4, 2048], P(None, 'hid'), may hold values from -3 to 3
- decay_down: bfloat16 [2048, 16], replicated, may hold values from -0.125 to 0.125
- decay_up: bfloat16 [16, 512], P(None, 'hid'), may hold values from -1.5 to 1.5
- decay_bias: float32 [512], P('hid'), may hold values from -2 to 10
- output_gate: bfloat16 [2048, 1024], P(None, 'hid'), may hold values from -0.125 to 0.125
- head_gain: bfloat16 [512], replicated, may hold values from 0.099609375 to 1.8984375
- output_weight: bfloat16 [1024, 2048], P('hid'), may hold values from -0.1875 to 0.1875
- mixer_gain: bfloat16 [2048], replicated, may hold values from 0.099609375 to 1.8984375
- gate_weight: bfloat16 [2048, 2816], P('req', 'hid'), may hold values from -0.125 to 0.125
- up_weight: bfloat16 [2048, 2816], P('req', 'hid'), may hold values from -0.125 to 0.125
- down_weight: bfloat16 [2816, 2048], P('hid', 'req'), may hold values from -0.109375 to 0.109375
- prompt_pages: int32 [16, 16], P('req'), may hold values from 0 to 64, as said below
- prompt_start: int32 [16, 16], P('req'), may hold values from 0 to 63, as said below
Outputs:
- hidden_out: bfloat16 [65536, 2048], P(('req', 'seq', 'hid'))
- page_states: bfloat16 [1024, 2, 256, 512], P(('req', 'seq'), 'hid')
- conv_edges: bfloat16 [1024, 3, 2048], P(('req', 'seq'), None, 'hid')
Inputs may be any that keep to these rules, and one draw needn't show every extreme that they name: `prompt_pages`: row r lists the page counts of the prompts of group r; 0 marks an unused slot; in every draw some group holds one prompt of all its 64 pages. `prompt_start`: the slots of a row that are used cover pages in increasing order without intersection and end by page 64; pages between prompts belong to none; an unused slot starts at page 64 - 1, and every draw has one.
All inputs are finite; a program needn't handle non-finite values.
Results may differ from a plain program's by a relative error of at most 0.014.
Values may be sent and summed in bfloat16 or wider, within the bound.
A program may use at most 192 MiB of HBM per device.

v0:
```python
import jax
import jax.numpy as jnp
from jax import lax
from jax.sharding import PartitionSpec as P

HK = 256
HV = 512
KCONV = 4
PAGE = 64
CONVW = 1024
EPSILON = 1e-06
TOP_PRECISION = lax.Precision.HIGHEST


def shifted(value, axis, steps):
    count = lax.axis_size(axis)
    first, last = (max(0, -steps), min(count, count - steps))
    return lax.ppermute(value, axis, [(source, source + steps) for source in range(first, last)])


def prefix_2(array, axis, join, neutral):
    place = lax.axis_index(axis)
    gathered = jax.tree.map(
        lambda a, kind: lax.all_gather(a.astype(kind), axis), array, (jnp.bfloat16, jnp.bfloat16)
    )
    state = jax.tree.map(lambda a, e: jnp.zeros_like(a) + jnp.asarray(e, a.dtype), array, neutral)

    def one(lap, state):
        return join(
            state,
            jax.tree.map(
                lambda a, own: lax.dynamic_index_in_dim(a, lap, 0, False).astype(own.dtype),
                gathered,
                array,
            ),
        )

    return lax.fori_loop(0, place, one, state)


def rms_scaled(values, scale_gain):
    values = values.astype(jnp.float32)
    return (
        values
        * lax.rsqrt(jnp.mean(values * values, axis=-1, keepdims=True) + EPSILON)
        * scale_gain.astype(jnp.float32)
    )


def page_segments(page_counts, starts, total_pages):
    position = jnp.arange(total_pages, dtype=jnp.int32)
    inside = (position[None, :] >= starts[:, None]) & (
        position[None, :] < starts[:, None] + page_counts[:, None]
    )
    labels = jnp.arange(1, page_counts.shape[0] + 1, dtype=jnp.int32)
    segment = jnp.sum(jnp.where(inside, labels[:, None], 0), axis=0) - 1
    earlier = jnp.concatenate([jnp.full((1,), -1, jnp.int32), segment[:-1]])
    return ((segment == earlier) & (segment >= 0)).astype(jnp.float32)


def short_conv(by_page, before, carried, conv_taps):
    kept_rows = before.astype(jnp.float32) * carried[:, None, None]
    widened = jnp.concatenate([kept_rows, by_page.astype(jnp.float32)], axis=1)
    tap_count = conv_taps.shape[0]
    length = by_page.shape[1]
    result = jnp.zeros(by_page.shape, jnp.float32)
    for offset in range(tap_count):
        result = (
            result
            + conv_taps[offset].astype(jnp.float32)
            * widened[:, tap_count - 1 - offset : tap_count - 1 - offset + length]
        )
    return result


def split_features(mixed_rows, key_width):
    query_rows = jax.nn.silu(mixed_rows[..., :key_width])
    key_rows = jax.nn.silu(mixed_rows[..., key_width : 2 * key_width]) * key_width ** (-0.5)
    value_matrix = mixed_rows[..., 2 * key_width :]
    return (
        query_rows.transpose(0, 2, 1, 3),
        key_rows.transpose(0, 2, 1, 3),
        value_matrix.transpose(0, 2, 1, 3),
    )


def page_step(memory_state, inputs):
    query_rows, key_rows, value_matrix, decay_sum, carried = inputs
    memory_state = memory_state * carried
    length = query_rows.shape[1]
    raised_rows = query_rows * jnp.exp(decay_sum)
    lowered = key_rows * jnp.exp(-decay_sum)
    scores = jnp.einsum("hik,hjk->hij", raised_rows, lowered, precision=TOP_PRECISION)
    rows_index = jnp.arange(length)
    causal = rows_index[:, None] >= rows_index[None, :]
    scores = jnp.where(causal[None], scores, 0.0)
    layer_output = jnp.einsum("hij,hjv->hiv", scores, value_matrix, precision=TOP_PRECISION)
    layer_output = layer_output + jnp.einsum(
        "eow,ews->eos", raised_rows, memory_state, precision=TOP_PRECISION
    )
    closing_sum = decay_sum[:, -1:, :]
    weighted_rows = key_rows * jnp.exp(closing_sum - decay_sum)
    memory_state = jnp.exp(closing_sum[:, 0, :])[:, :, None] * memory_state + jnp.einsum(
        "lte,ltb->leb", weighted_rows, value_matrix, precision=TOP_PRECISION
    )
    return (memory_state, (layer_output, memory_state))


def on_device(
    tokens,
    attention_gain,
    project_weight,
    conv_weight,
    decay_down,
    decay_up,
    decay_bias,
    output_gate,
    head_gain,
    output_weight,
    mixer_gain,
    gate_weight,
    up_weight,
    down_weight,
    prompt_pages,
    prompt_start,
):
    token_count = tokens.shape[0]
    page_count = token_count // PAGE
    local_heads = project_weight.shape[1] // CONVW
    rim_rows = KCONV - 1
    seq_index = lax.axis_index("seq")
    group_pages = page_count * lax.axis_size("seq")
    page_flags = page_segments(prompt_pages[0], prompt_start[0], group_pages)
    carried = lax.dynamic_slice_in_dim(page_flags, seq_index * page_count, page_count)
    normed = rms_scaled(tokens, attention_gain).astype(jnp.bfloat16)
    projected = jnp.dot(normed, project_weight, preferred_element_type=jnp.float32).astype(
        jnp.bfloat16
    )
    by_page = projected.reshape(page_count, PAGE, local_heads * CONVW)
    incoming = shifted(by_page[-1, PAGE - rim_rows :], "seq", 1)
    before = jnp.concatenate([incoming[None], by_page[:-1, PAGE - rim_rows :]], axis=0)
    mixed_rows = short_conv(by_page, before, carried, conv_weight).reshape(
        page_count, PAGE, local_heads, CONVW
    )
    query_rows, key_rows, value_matrix = split_features(mixed_rows, HK)
    lowrank = jnp.dot(normed, decay_down, preferred_element_type=jnp.float32).astype(jnp.bfloat16)
    decay_log = (
        jax.nn.log_sigmoid(
            jnp.dot(lowrank, decay_up, preferred_element_type=jnp.float32) + decay_bias
        )
        / 16.0
    )
    decay_log = decay_log.reshape(page_count, PAGE, local_heads, HK).transpose(0, 2, 1, 3)
    decay_sum = jnp.cumsum(decay_log, axis=2)
    start_memory = jnp.zeros((local_heads, HK, HV), jnp.float32)
    local_memory, (outputs, memories) = lax.scan(
        page_step, start_memory, (query_rows, key_rows, value_matrix, decay_sum, carried)
    )
    totals = decay_sum[:, :, -1, :]
    through = jnp.cumsum(totals, axis=0)
    alive_mask = jnp.cumprod(carried)
    block_decay = alive_mask[-1] * jnp.exp(through[-1])

    def compose(earlier, latter):
        return (earlier[0] * latter[0], latter[0][..., None] * earlier[1] + latter[1])

    prefix = prefix_2(
        (block_decay, local_memory),
        "seq",
        compose,
        (jnp.ones_like(block_decay), jnp.zeros_like(local_memory)),
    )
    incoming_state = prefix[1]
    before_sum = through - totals
    extent_factor = alive_mask[:, None, None, None] * jnp.exp(decay_sum + before_sum[:, :, None, :])
    outputs = outputs + jnp.einsum(
        "dlof,lfg->dlog", query_rows * extent_factor, incoming_state, precision=TOP_PRECISION
    )
    memories = (
        memories + (alive_mask[:, None, None] * jnp.exp(through))[..., None] * incoming_state[None]
    )
    attended = outputs.transpose(0, 2, 1, 3).reshape(token_count, local_heads, HV)
    normed_heads = rms_scaled(attended, head_gain)
    opening = jax.nn.silu(jnp.dot(normed, output_gate, preferred_element_type=jnp.float32)).reshape(
        token_count, local_heads, HV
    )
    gated_rows = (
        (normed_heads * opening).astype(jnp.bfloat16).reshape(token_count, local_heads * HV)
    )
    partial_value = jnp.dot(gated_rows, output_weight, preferred_element_type=jnp.float32)
    half_rows = token_count // lax.axis_size("hid")
    row_start = lax.axis_index("hid") * half_rows
    mixed_sum = lax.psum(partial_value.astype(jnp.bfloat16), "hid").astype(jnp.float32)
    residual = (tokens.astype(jnp.float32) + mixed_sum).astype(jnp.bfloat16)
    feed_in = rms_scaled(residual, mixer_gain).astype(jnp.bfloat16)
    own_residual = lax.dynamic_slice_in_dim(residual, row_start, half_rows, 0)

    def widen(weight_rows):
        return jnp.dot(feed_in, weight_rows, preferred_element_type=jnp.float32)

    gate_part = widen(lax.all_gather(gate_weight, "req", axis=0, tiled=True))
    up_part = widen(lax.all_gather(up_weight, "req", axis=0, tiled=True))
    hidden = (jax.nn.silu(gate_part) * up_part).astype(jnp.bfloat16)
    partials = jnp.dot(
        hidden,
        lax.all_gather(down_weight, "req", axis=1, tiled=True),
        preferred_element_type=jnp.float32,
    )
    feed_sum = lax.psum_scatter(
        partials.astype(jnp.bfloat16), "hid", scatter_dimension=0, tiled=True
    ).astype(jnp.float32)
    result = (own_residual.astype(jnp.float32) + feed_sum).astype(jnp.bfloat16)
    return (result, memories.astype(jnp.bfloat16), by_page[:, PAGE - rim_rows :])


def solution(mesh):
    return jax.shard_map(
        on_device,
        mesh=mesh,
        in_specs=(
            P(("req", "seq"), None),
            P(),
            P(None, "hid"),
            P(None, "hid"),
            P(),
            P(None, "hid"),
            P("hid"),
            P(None, "hid"),
            P(),
            P("hid", None),
            P(),
            P("req", "hid"),
            P("req", "hid"),
            P("hid", "req"),
            P("req", None),
            P("req", None),
        ),
        out_specs=(
            P(("req", "seq", "hid"), None),
            P(("req", "seq"), "hid", None, None),
            P(("req", "seq"), None, "hid"),
        ),
        check_vma=False,
    )
```

profile of v0, /device:TPU:1, one launch (start us, length us, event | category | flops | bytes accessed | tf_op | source)
XLA Modules:
  0.0 471.6 jit_solution(12928191912061938082)
XLA Ops:
  8.1 3.2 fusion.29
  11.6 7.2 %convolution_convert_fusion.2 = bf16[1024,1024]{1,0:T(8,128)(2,1)S(1)} fusion(bf16[2048,1024]{1,0:T(8,128)(2,1)} %param.22, bf16[1024,2048]{1,0:T(8,128)(2,1)S(1)} %copy-done.2, f32[2048]{0:T(1024)S(1)} %convert_element_type.146, f32[1024]{0:T(1024)S(1)} %add_rsqrt_fusion.2), kind=kOutput, calls=%fused_computation.78 | convolution fusion | flops 4304404480 | bytes 10498048 | tf_op jit(solution)/shard_map/dot_general | solution.py:136
  18.9 4.5 collective-permute-start
  23.5 3.2 copy_convert_fusion
  26.9 4.2 fusion.50
  34.4 7.3 %fusion.37 = f32[16,64,1,1024]{3,0,1,2:T(8,128)S(1)} fusion(f32[16,64,1024]{2,0,1:T(8,128)} %copy_convert_fusion, f32[16,3,1024]{2,0,1:T(8,128)S(1)} %convert_multiply_fusion.4, f32[1024]{0:T(1024)S(1)} %bitcast.168, f32[1024]{0:T(1024)S(1)} %bitcast.169, f32[1024]{0:T(1024)S(1)} %bitcast.167, f32[1024]{0:T(1024)S(1)} %bitcast.166), kind=kLoop, calls=%fused_computation.61 | loop fusion | flops 10485760 | bytes 8601600 | tf_op jit(solution)/shard_map/reshape | solution.py:142
  41.7 1.6 slice_bitcast_fusion
  43.3 2.1 fusion.54
  45.4 143.3 %while.28 = (s32[]{:T(128)}, f32[1,256,512]{2,1,0:T(8,128)S(1)}, f32[16,1,64,512]{3,2,1,0:T(8,128)}, f32[16,1,256,512]{3,2,1,0:T(8,128)}, f32[16,1,64,256]{3,0,1...) while((s32[]{:T(128)}, f32[1,256,512]{2,1,0:T(8,128)S(1)}, ...), condition=%wide.region_4.5_spmd.clone, body=%wide.region_3.4_spmd.clone.sunk | while | flops 240001024 | bytes 4038800 | solution.py:156
  48.0 1.3 constant_dynamic-slice_fusion.7
  50.3 1.8 fusion.107
  52.2 2.2 bitcast_dynamic-update-slice_fusion.2
  57.0 1.3 constant_dynamic-slice_fusion.7
  59.3 1.8 fusion.107
  61.1 2.2 bitcast_dynamic-update-slice_fusion.2
  65.9 1.3 constant_dynamic-slice_fusion.7
  68.2 1.8 fusion.107
  70.1 2.2 bitcast_dynamic-update-slice_fusion.2
  74.9 1.3 constant_dynamic-slice_fusion.7
  77.2 1.8 fusion.107
  79.0 2.2 bitcast_dynamic-update-slice_fusion.2
  83.9 1.3 constant_dynamic-slice_fusion.7
  86.2 1.8 fusion.107
  88.0 2.2 bitcast_dynamic-update-slice_fusion.2
  95.1 1.8 fusion.107
  97.0 2.2 bitcast_dynamic-update-slice_fusion.2
  104.1 1.8 fusion.107
  105.9 2.2 bitcast_dynamic-update-slice_fusion.2
  110.7 1.3 constant_dynamic-slice_fusion.7
  113.0 1.8 fusion.107
  114.9 2.2 bitcast_dynamic-update-slice_fusion.2
  122.0 1.8 fusion.107
  123.8 2.2 bitcast_dynamic-update-slice_fusion.2
  130.9 1.8 fusion.107
  132.7 2.2 bitcast_dynamic-update-slice_fusion.2
  139.9 1.8 fusion.107
  141.7 2.2 bitcast_dynamic-update-slice_fusion.2
  148.8 1.8 fusion.107
  150.7 2.2 bitcast_dynamic-update-slice_fusion.2
  155.5 1.3 constant_dynamic-slice_fusion.7
  157.8 1.8 fusion.107
  159.6 2.2 bitcast_dynamic-update-slice_fusion.2
  164.5 1.3 constant_dynamic-slice_fusion.7
  166.7 1.8 fusion.107
  168.6 2.2 bitcast_dynamic-update-slice_fusion.2
  175.7 1.8 fusion.107
  177.5 2.2 bitcast_dynamic-update-slice_fusion.2
  184.6 1.8 fusion.107
  186.5 2.2 bitcast_dynamic-update-slice_fusion.2
  190.8 6.9 %all_gather.19 = bf16[4,1,256]{2,1,0:T(2,128)(2,1)S(1)} all-gather(bf16[1,1,256]{2,1,0:T(2,128)(2,1)S(1)} %fusion.65), channel_id=1, replica_groups=mesh['req'=16,'seq'=4,'hid'=2] {'seq'}, dimensions={0}, use_global_device_ids=true | all-gather | bytes 2560 | tf_op jit(solution)/shard_map/all_gather | solution.py:24
  197.7 17.4 %all-gather.12.cloned.1.call-done = bf16[4,256,512]{2,1,0:T(8,128)(2,1)} async-done(((bf16[1,256,512]{2,1,0:T(8,128)(2,1)}), bf16[4,256,512]{2,1,0:T(8,128)(2,1)}) %all-gather.12.cloned.1.call-update) | async-done | bytes 1048592 | tf_op jit(solution)/shard_map/all_gather | solution.py:24
  215.4 5.6 %multiply_reduce_fusion = (f32[16,64]{1,0:T(8,128)S(1)}, f32[16,1,64,512]{3,2,0,1:T(8,128)}) fusion(f32[16,64,256]{2,0,1:T(8,128)} %get-tuple-element.223, f32[1,256,512]{2,1,0:T(8,128)S(1)} %get-tuple-element.98, f32[16,1,64,512]{3,2,1,0:T(8,128)} %get-tuple-element.96), kind=kOutput, calls=%fused_computation.77 | convolution fusion | flops 1612184576 | bytes 5771264 | tf_op jit(solution)/shard_map/dlof,lfg->dlog/dot_general | solution.py:176
  221.1 6.2 %fusion.44 = bf16[1024,512]{1,0:T(8,128)(2,1)S(1)} fusion(f32[16,1,64,512]{3,2,0,1:T(8,128)} %get-tuple-element.231, f32[512]{0:T(512)S(1)} %convert_element_type.163, f32[1024]{0:T(1024)S(1)} %rsqrt.29, bf16[2048,512]{1,0:T(8,128)(2,1)} %param.27, bf16[1024,2048]{1,0:T(8,128)(2,1)} %param.20, f32[2048]{0:T(1024)S(1)} %convert_element_type.146, ...), kind=kOutput, calls=%fused_computation.76 | convolution fusion | flops 2160066560 | bytes 9455616 | tf_op jit(solution)/shard_map/dot_general | solution.py:184
  227.2 4.4 convolution_convert_fusion.1
  233.7 36.6 %all-reduce.2.cloned.1.call-done = bf16[1024,2048]{1,0:T(8,128)(2,1)} async-done(((bf16[1024,2048]{1,0:T(8,128)(2,1)}), bf16[1024,2048]{1,0:T(8,128)(2,1)}) %all-reduce.2.cloned.1.call-update) | async-done | bytes 4194320 | tf_op jit(solution)/shard_map/psum | solution.py:193
  270.3 7.7 %fusion.26 = (f32[1024]{0:T(1024)S(1)}, bf16[1024,2048]{1,0:T(8,128)(2,1)}) fusion(bf16[1024,2048]{1,0:T(8,128)(2,1)} %all-reduce.2.cloned.1.call-done, bf16[1024,2048]{1,0:T(8,128)(2,1)} %param.20), kind=kLoop, calls=%fused_computation.44 | loop fusion | flops 14679040 | bytes 12587008 | tf_op jit(solution)/shard_map/reduce_sum | solution.py:45
  278.0 19.1 %all-gather.6.cloned.1.call-done = bf16[2048,1408]{1,0:T(8,128)(2,1)} async-done(((bf16[128,1408]{1,0:T(8,128)(2,1)}), bf16[2048,1408]{1,0:T(8,128)(2,1)}) %all-gather.6.cloned.1.call-update) | async-done | bytes 5767184 | tf_op jit(solution)/shard_map/all_gather | solution.py:201
  297.1 12.0 %fusion.47 = f32[1024,1408]{1,0:T(8,128)} fusion(bf16[2048,1408]{1,0:T(8,128)(2,1)} %all-gather.6.cloned.1.call-done, bf16[1024,2048]{1,0:T(8,128)(2,1)} %get-tuple-element.218, f32[2048]{0:T(1024)S(1)} %convert_element_type.170, f32[1024]{0:T(1024)S(1)} %add_rsqrt_fusion.1), kind=kOutput, calls=%fused_computation.81 | convolution fusion | flops 5913968640 | bytes 15740928 | tf_op jit(solution)/shard_map/dot_general | solution.py:199
  309.0 53.5 %all-gather.10.cloned.1.call-done = bf16[1408,2048]{1,0:T(8,128)(2,1)} async-done(((bf16[1408,128]{1,0:T(8,128)(2,1)}), bf16[1408,2048]{1,0:T(8,128)(2,1)}) %all-gather.10.cloned.1.call-update) | async-done | bytes 5767184 | tf_op jit(solution)/shard_map/all_gather | solution.py:206
  362.5 61.3 %all-gather.8.cloned.1.call-done = bf16[2048,1408]{1,0:T(8,128)(2,1)} async-done(((bf16[128,1408]{1,0:T(8,128)(2,1)}), bf16[2048,1408]{1,0:T(8,128)(2,1)}) %all-gather.8.cloned.1.call-update) | async-done | bytes 5767184 | tf_op jit(solution)/shard_map/all_gather | solution.py:202
  423.8 20.9 %convolution_convert_fusion = bf16[1024,2048]{1,0:T(8,128)(2,1)} fusion(bf16[1408,2048]{1,0:T(8,128)(2,1)} %all-gather.10.cloned.1.call-done, f32[1024,1408]{1,0:T(8,128)} %fusion.47, bf16[2048,1408]{1,0:T(8,128)(2,1)} %all-gather.8.cloned.1.call-done, bf16[1024,2048]{1,0:T(8,128)(2,1)} %get-tuple-element.218, f32[2048]{0:T(1024)S(1)} %convert_element_type.170, ...), kind=kOutput, calls=%fused_computation.68 | convolution fusion | flops 11830296576 | bytes 25702400 | tf_op jit(solution)/shard_map/dot_general | solution.py:204
  446.5 5.4 %add_convert_fusion = bf16[16,1,256,512]{3,2,1,0:T(8,128)(2,1)} fusion(f32[16,1,256,512]{3,2,1,0:T(8,128)} %get-tuple-element.99, f32[256,512]{1,0:T(8,128)S(1)} %bitcast.155, f32[16,256]{1,0:T(8,128)S(1)} %bitcast_multiply_fusion.1), kind=kLoop, calls=%fused_computation.51 | loop fusion | flops 6291456 | bytes 13123584 | tf_op jit(solution)/shard_map/convert_element_type | solution.py:213
  451.8 7.9 %reduce-scatter.2.cloned.1.call-done = bf16[512,2048]{1,0:T(8,128)(2,1)} async-done(((bf16[1024,2048]{1,0:T(8,128)(2,1)}), bf16[512,2048]{1,0:T(8,128)(2,1)}) %reduce-scatter.2.cloned.1.call-update) | async-done | bytes 2097168 | tf_op jit(solution)/shard_map/reduce_scatter | solution.py:209
  459.8 4.4 add_convert_fusion.1
  (216 shorter events, 77.6 us)
Async XLA Ops:
  8.0 219.2 %copy-start = (bf16[512,2048]{1,0:T(8,128)(2,1)S(1)}, bf16[512,2048]{1,0:T(8,128)(2,1)}, u32[]{:S(2)}) copy-start(bf16[512,2048]{1,0:T(8,128)(2,1)} %param.29) | copy-start | bytes 6291460
  8.0 3.3 copy-start.7
  8.0 207.1 %all-gather.12.cloned.1.call-start = ((), (), s32[]{:S(2)}) async-start(), calls=%async_computation.6 | async-start | bytes 1310720 | tf_op jit(solution)/shard_map/all_gather | solution.py:24
  8.1 3.6 copy-start.2
  18.8 4.6 copy-start.5
  18.8 7.8 %copy-start.9 = (s32[1,16]{1,0:T(1,128)S(1)}, s32[1,16]{1,0:T(1,128)}, u32[]{:S(2)}) copy-start(s32[1,16]{1,0:T(1,128)} %param.35) | copy-start | bytes 196
  18.9 7.8 %copy-start.11 = (s32[1,16]{1,0:T(1,128)S(1)}, s32[1,16]{1,0:T(1,128)}, u32[]{:S(2)}) copy-start(s32[1,16]{1,0:T(1,128)} %param.34) | copy-start | bytes 196
  18.9 7.9 %copy-start.6 = (bf16[4,1024]{1,0:T(4,128)(2,1)S(1)}, bf16[4,1024]{1,0:T(4,128)(2,1)}, u32[]{:S(2)}) copy-start(bf16[4,1024]{1,0:T(4,128)(2,1)} %param.23) | copy-start | bytes 24580
  18.9 8.0 %copy-start.12 = (bf16[2048,16]{0,1:T(8,128)(2,1)S(1)}, bf16[2048,16]{0,1:T(8,128)(2,1)}, u32[]{:S(2)}) copy-start(bf16[2048,16]{0,1:T(8,128)(2,1)} %param.24) | copy-start | bytes 196612
  18.9 8.0 %copy-start.13 = (bf16[16,256]{1,0:T(8,128)(2,1)S(1)}, bf16[16,256]{1,0:T(8,128)(2,1)}, u32[]{:S(2)}) copy-start(bf16[16,256]{1,0:T(8,128)(2,1)} %param.25) | copy-start | bytes 24580
  18.9 7.9 %copy-start.14 = (f32[256]{0:T(256)S(1)}, f32[256]{0:T(256)}, u32[]{:S(2)}) copy-start(f32[256]{0:T(256)} %param.26) | copy-start | bytes 3076
  18.9 15.4 %collective-permute-start = (bf16[3,1024]{1,0:T(4,128)(2,1)S(1)}, bf16[3,1024]{1,0:T(4,128)(2,1)S(1)}, u32[]{:S(2)}, u32[]{:S(2)}) collective-permute-start(bf16[3,1024]{1,0:T(4,128)(2,1)S(1)} %slice_bitcast_fusion.2), channel_id=1, source_target_pairs={{0,2},{2,4},{4,6},{1,3},{3,5},{5,7},{8,10},{10,12},{12,14},{9,11},... | collective-permute-start | bytes 18440 | tf_op jit(solution)/shard_map/ppermute | solution.py:18
  31.7 1.0 copy-start.3
  41.7 1.6 copy-start.4
  45.4 144.7 %copy-start.10 = (bf16[512]{0:T(512)(128)(2,1)S(1)}, bf16[512]{0:T(512)(128)(2,1)}, u32[]{:S(2)}) copy-start(bf16[512]{0:T(512)(128)(2,1)} %param.28) | copy-start | bytes 3076
  189.5 80.8 %all-reduce.2.cloned.1.call-start = ((), (), s32[]{:S(2)}) async-start(), calls=%async_computation.1 | async-start | bytes 8388608 | tf_op jit(solution)/shard_map/psum | solution.py:193
  231.6 2.0 copy-start.8
  231.6 65.5 %all-gather.6.cloned.1.call-start = ((), (), s32[]{:S(2)}) async-start(), calls=%async_computation.2 | async-start | bytes 6127616 | tf_op jit(solution)/shard_map/all_gather | solution.py:201
  232.2 130.3 %all-gather.10.cloned.1.call-start = ((), (), s32[]{:S(2)}) async-start(), calls=%async_computation.4 | async-start | bytes 6127616 | tf_op jit(solution)/shard_map/all_gather | solution.py:206
  232.8 191.0 %all-gather.8.cloned.1.call-start = ((), (), s32[]{:S(2)}) async-start(), calls=%async_computation.3 | async-start | bytes 6127616 | tf_op jit(solution)/shard_map/all_gather | solution.py:202
  233.4 226.4 %reduce-scatter.2.cloned.1.call-start = ((), (), s32[]{:S(2)}) async-start(), calls=%async_computation.5 | async-start | bytes 6291456 | tf_op jit(solution)/shard_map/reduce_scatter | solution.py:209
  446.5 17.8 %copy-start.1 = (bf16[512,2048]{1,0:T(8,128)(2,1)S(1)}, bf16[512,2048]{1,0:T(8,128)(2,1)}, u32[]{:S(2)}) copy-start(bf16[512,2048]{1,0:T(8,128)(2,1)} %param.29) | copy-start | bytes 6291460
Sparse Core Ops, SparseCore 0:
  189.6 25.4 all-gather.11
  231.7 38.5 all-reduce.1
  444.8 14.9 reduce-scatter.1
Sparse Core Ops, SparseCore 1:
  234.4 62.6 all-gather.5
  299.3 63.2 all-gather.9
  364.7 59.0 all-gather.7
where the time goes:
time: 474 us; the launch traced here: 472 us
  waiting for transfers between devices  197 us (42%)
  matrix products  132 us (28%)
  local copies, waits for them, and re-layouts  77.3 us (16%)
  other arithmetic  36 us (8%)
  between operations  15.8 us (3%)
  blocking collectives  6.89 us (1%)
  starting transfers between devices  4.97 us (1%)
    dynamic_slice x80, local copies, waits for them, and re-layouts, on_device(): lax.scan(page_step, start_memory, (query_rows, key_rows, value_matrix, de...  70.5 us
    all_gather x1, waiting for transfers between devices, on_device(): up_part = widen(lax.all_gather(up_weight, 'req', axis=0, tiled=True))  61.3 us
    all_gather x1, waiting for transfers between devices, on_device(): lax.all_gather(down_weight, 'req', axis=1, tiled=True)  53.5 us
    psum x1, waiting for transfers between devices, on_device(): lax.psum(partial_value.astype(jnp.bfloat16), 'hid').astype(jnp.float32)  36.6 us
    dot_general x16, matrix products, page_step(): jnp.einsum('lte,ltb->leb', weighted_rows, value_matrix, precision=TOP_PRE...  35.4 us
    dot_general x16, matrix products, page_step(): jnp.einsum('eow,ews->eos', raised_rows, memory_state, precision=TOP_PRECI...  29 us
    dot_general x1, matrix products, on_device(): jnp.dot(hidden, lax.all_gather(down_weight, 'req', axis=1, tiled=True), p...  20.9 us
    all_gather x1, waiting for transfers between devices, on_device(): gate_part = widen(lax.all_gather(gate_weight, 'req', axis=0, tiled=True))  19.1 us
  transfers between devices with their start and end apart: 7, of which 6 were waited for; matrix products, arithmetic and copies ran while one was open for 8% of the time, Pallas kernels for 0%

commit v1 on v0

--- a/solution.py
+++ b/solution.py
@@ -190,7 +190,9 @@
     partial_value = jnp.dot(gated_rows, output_weight, preferred_element_type=jnp.float32)
     half_rows = token_count // lax.axis_size("hid")
     row_start = lax.axis_index("hid") * half_rows
-    mixed_sum = lax.psum(partial_value.astype(jnp.bfloat16), "hid").astype(jnp.float32)
+    mixed_sum = jnp.sum(lax.all_gather(partial_value.astype(jnp.bfloat16), "hid"), axis=0).astype(
+        jnp.float32
+    )
     residual = (tokens.astype(jnp.float32) + mixed_sum).astype(jnp.bfloat16)
     feed_in = rms_scaled(residual, mixer_gain).astype(jnp.bfloat16)
     own_residual = lax.dynamic_slice_in_dim(residual, row_start, half_rows, 0)

time: 474 us -> 497 us (1.049)
  waiting for transfers between devices: 197 us -> 213 us
  other arithmetic: 36 us -> 44.6 us
    psum x1 -> x0, waiting for transfers between devices: 36.6 us -> none  [on_device(): lax.psum(partial_value.astype(jnp.bfloat16), 'hid').astype(jnp.float32)]
    all_gather x1, waiting for transfers between devices: 19.1 us -> 45.5 us  [on_device(): gate_part = widen(lax.all_gather(gate_weight, 'req', axis=0, tiled=True))]
    all_gather x0 -> x1, waiting for transfers between devices: none -> 25.3 us  [on_device(): lax.all_gather(partial_value.astype(jnp.bfloat16), 'hid')]
    all_gather x1, waiting for transfers between devices: 61.3 us -> 48.5 us  [on_device(): up_part = widen(lax.all_gather(up_weight, 'req', axis=0, tiled=True))]
    all_gather x1, waiting for transfers between devices: 53.5 us -> 65.9 us  [on_device(): lax.all_gather(down_weight, 'req', axis=1, tiled=True)]
    reduce_sum x0 -> x1, other arithmetic: none -> 8.78 us  [on_device(): jnp.sum(lax.all_gather(partial_value.astype(jnp.bfloat16), 'hid'), axis=0)]
  transfers between devices with their start and end apart: 7 -> 7, of which waited for: 6 -> 6; matrix products, arithmetic and copies ran while one was open for 8% -> 9% of each run, Pallas kernels for 0% -> 0%
where the time goes in v1:
time: 497 us; the launch traced here: 494 us
  waiting for transfers between devices  213 us (43%)
  matrix products  133 us (27%)
  local copies, waits for them, and re-layouts  77.3 us (16%)
  other arithmetic  44.6 us (9%)
  between operations  14.5 us (3%)
  blocking collectives  6.89 us (1%)
    dynamic_slice x80, local copies, waits for them, and re-layouts, on_device(): lax.scan(page_step, start_memory, (query_rows, key_rows, value_matrix, de...  70.5 us
    all_gather x1, waiting for transfers between devices, on_device(): lax.all_gather(down_weight, 'req', axis=1, tiled=True)  65.9 us
    all_gather x1, waiting for transfers between devices, on_device(): up_part = widen(lax.all_gather(up_weight, 'req', axis=0, tiled=True))  48.5 us
    all_gather x1, waiting for transfers between devices, on_device(): gate_part = widen(lax.all_gather(gate_weight, 'req', axis=0, tiled=True))  45.5 us
    dot_general x16, matrix products, page_step(): jnp.einsum('lte,ltb->leb', weighted_rows, value_matrix, precision=TOP_PRE...  35.4 us
    dot_general x16, matrix products, page_step(): jnp.einsum('eow,ews->eos', raised_rows, memory_state, precision=TOP_PRECI...  29 us
    all_gather x1, waiting for transfers between devices, on_device(): lax.all_gather(partial_value.astype(jnp.bfloat16), 'hid')  25.3 us
    dot_general x1, matrix products, on_device(): jnp.dot(hidden, lax.all_gather(down_weight, 'req', axis=1, tiled=True), p...  20.9 us
  transfers between devices with their start and end apart: 7, of which 6 were waited for; matrix products, arithmetic and copies ran while one was open for 9% of the time, Pallas kernels for 0%

profile of v1, /device:TPU:1, one launch (start us, length us, event | category | flops | bytes accessed | tf_op | source)
XLA Modules:
  0.0 494.0 jit_solution(14421341568843880836)
XLA Ops:
  7.2 3.2 fusion.29
  10.8 7.2 %convolution_convert_fusion.2 = bf16[1024,1024]{1,0:T(8,128)(2,1)S(1)} fusion(bf16[2048,1024]{1,0:T(8,128)(2,1)} %param.22, bf16[1024,2048]{1,0:T(8,128)(2,1)S(1)} %copy-done.2, f32[2048]{0:T(1024)S(1)} %convert_element_type.148, f32[1024]{0:T(1024)S(1)} %add_rsqrt_fusion.2), kind=kOutput, calls=%fused_computation.78 | convolution fusion | flops 4304404480 | bytes 10498048 | tf_op jit(solution)/shard_map/dot_general | solution.py:136
  18.1 4.5 collective-permute-start
  22.6 3.2 copy_convert_fusion
  26.0 4.2 fusion.50
  33.6 7.3 %fusion.37 = f32[16,64,1,1024]{3,0,1,2:T(8,128)S(1)} fusion(f32[16,64,1024]{2,0,1:T(8,128)} %copy_convert_fusion, f32[16,3,1024]{2,0,1:T(8,128)S(1)} %convert_multiply_fusion.4, f32[1024]{0:T(1024)S(1)} %bitcast.170, f32[1024]{0:T(1024)S(1)} %bitcast.171, f32[1024]{0:T(1024)S(1)} %bitcast.169, f32[1024]{0:T(1024)S(1)} %bitcast.168), kind=kLoop, calls=%fused_computation.61 | loop fusion | flops 10485760 | bytes 8601600 | tf_op jit(solution)/shard_map/reshape | solution.py:142
  40.9 1.6 slice_bitcast_fusion
  42.5 2.1 fusion.54
  44.6 143.3 %while.28 = (s32[]{:T(128)}, f32[1,256,512]{2,1,0:T(8,128)S(1)}, f32[16,1,64,512]{3,2,1,0:T(8,128)}, f32[16,1,256,512]{3,2,1,0:T(8,128)}, f32[16,1,64,256]{3,0,1...) while((s32[]{:T(128)}, f32[1,256,512]{2,1,0:T(8,128)S(1)}, ...), condition=%wide.region_4.5_spmd.clone, body=%wide.region_3.4_spmd.clone.sunk | while | flops 240001024 | bytes 4038800 | solution.py:156
  47.2 1.3 constant_dynamic-slice_fusion.7
  49.5 1.8 fusion.107
  51.3 2.2 bitcast_dynamic-update-slice_fusion.2
  56.1 1.3 constant_dynamic-slice_fusion.7
  58.4 1.8 fusion.107
  60.3 2.2 bitcast_dynamic-update-slice_fusion.2
  65.1 1.3 constant_dynamic-slice_fusion.7
  67.4 1.8 fusion.107
  69.2 2.2 bitcast_dynamic-update-slice_fusion.2
  74.1 1.3 constant_dynamic-slice_fusion.7
  76.4 1.8 fusion.107
  78.2 2.2 bitcast_dynamic-update-slice_fusion.2
  83.0 1.3 constant_dynamic-slice_fusion.7
  85.3 1.8 fusion.107
  87.2 2.2 bitcast_dynamic-update-slice_fusion.2
  92.0 1.3 constant_dynamic-slice_fusion.7
  94.3 1.8 fusion.107
  96.1 2.2 bitcast_dynamic-update-slice_fusion.2
  103.2 1.8 fusion.107
  105.1 2.2 bitcast_dynamic-update-slice_fusion.2
  112.2 1.8 fusion.107
  114.0 2.2 bitcast_dynamic-update-slice_fusion.2
  121.1 1.8 fusion.107
  123.0 2.2 bitcast_dynamic-update-slice_fusion.2
  127.8 1.3 constant_dynamic-slice_fusion.7
  130.1 1.8 fusion.107
  131.9 2.2 bitcast_dynamic-update-slice_fusion.2
  139.0 1.8 fusion.107
  140.9 2.2 bitcast_dynamic-update-slice_fusion.2
  148.0 1.8 fusion.107
  149.8 2.2 bitcast_dynamic-update-slice_fusion.2
  157.0 1.8 fusion.107
  158.8 2.2 bitcast_dynamic-update-slice_fusion.2
  165.9 1.8 fusion.107
  167.7 2.2 bitcast_dynamic-update-slice_fusion.2
  174.8 1.8 fusion.107
  176.7 2.2 bitcast_dynamic-update-slice_fusion.2
  183.8 1.8 fusion.107
  185.6 2.2 bitcast_dynamic-update-slice_fusion.2
  190.0 6.9 %all_gather.25 = bf16[4,1,256]{2,1,0:T(2,128)(2,1)S(1)} all-gather(bf16[1,1,256]{2,1,0:T(2,128)(2,1)S(1)} %fusion.65), channel_id=1, replica_groups=mesh['req'=16,'seq'=4,'hid'=2] {'seq'}, dimensions={0}, use_global_device_ids=true | all-gather | bytes 2560 | tf_op jit(solution)/shard_map/all_gather | solution.py:24
  196.9 17.4 %all-gather.14.cloned.1.call-done = bf16[4,256,512]{2,1,0:T(8,128)(2,1)} async-done(((bf16[1,256,512]{2,1,0:T(8,128)(2,1)}), bf16[4,256,512]{2,1,0:T(8,128)(2,1)}) %all-gather.14.cloned.1.call-update) | async-done | bytes 1048592 | tf_op jit(solution)/shard_map/all_gather | solution.py:24
  214.5 5.6 %multiply_reduce_fusion = (f32[16,64]{1,0:T(8,128)S(1)}, f32[16,1,64,512]{3,2,0,1:T(8,128)}) fusion(f32[16,64,256]{2,0,1:T(8,128)} %get-tuple-element.223, f32[1,256,512]{2,1,0:T(8,128)S(1)} %get-tuple-element.98, f32[16,1,64,512]{3,2,1,0:T(8,128)} %get-tuple-element.96), kind=kOutput, calls=%fused_computation.77 | convolution fusion | flops 1612184576 | bytes 5771264 | tf_op jit(solution)/shard_map/dlof,lfg->dlog/dot_general | solution.py:176
  220.2 6.2 %fusion.44 = bf16[1024,512]{1,0:T(8,128)(2,1)S(1)} fusion(f32[16,1,64,512]{3,2,0,1:T(8,128)} %get-tuple-element.231, f32[512]{0:T(512)S(1)} %convert_element_type.165, f32[1024]{0:T(1024)S(1)} %rsqrt.29, bf16[2048,512]{1,0:T(8,128)(2,1)} %param.27, bf16[1024,2048]{1,0:T(8,128)(2,1)} %param.20, f32[2048]{0:T(1024)S(1)} %convert_element_type.148, ...), kind=kOutput, calls=%fused_computation.76 | convolution fusion | flops 2160066560 | bytes 9455616 | tf_op jit(solution)/shard_map/dot_general | solution.py:184
  226.4 4.4 convolution_convert_fusion.1
  232.7 25.3 %all-gather.16.cloned.1.call-done = bf16[2048,2048]{1,0:T(8,128)(2,1)} async-done(((bf16[1024,2048]{1,0:T(8,128)(2,1)}), bf16[2048,2048]{1,0:T(8,128)(2,1)}) %all-gather.16.cloned.1.call-update) | async-done | bytes 8388624 | tf_op jit(solution)/shard_map/all_gather | solution.py:193
  258.0 8.8 %reduce_sum.51 = bf16[1024,2048]{1,0:T(8,128)(2,1)} reduce(bf16[2,1024,2048]{2,1,0:T(8,128)(2,1)} %bitcast.157, bf16[]{:T(256)} %constant.97.clone.1), dimensions={0}, to_apply=%region_10.11 | reduce | flops 2097152 | bytes 12582914 | tf_op jit(solution)/shard_map/reduce_sum | solution.py:193
  266.8 7.5 %fusion.26 = (f32[1024]{0:T(1024)S(1)}, bf16[1024,2048]{1,0:T(8,128)(2,1)}) fusion(bf16[1024,2048]{1,0:T(8,128)(2,1)} %reduce_sum.51, bf16[1024,2048]{1,0:T(8,128)(2,1)} %param.20), kind=kLoop, calls=%fused_computation.44 | loop fusion | flops 14679040 | bytes 12587008 | tf_op jit(solution)/shard_map/reduce_sum | solution.py:45
  274.3 45.5 %all-gather.8.cloned.1.call-done = bf16[2048,1408]{1,0:T(8,128)(2,1)} async-done(((bf16[128,1408]{1,0:T(8,128)(2,1)}), bf16[2048,1408]{1,0:T(8,128)(2,1)}) %all-gather.8.cloned.1.call-update) | async-done | bytes 5767184 | tf_op jit(solution)/shard_map/all_gather | solution.py:203
  319.8 12.0 %fusion.47 = f32[1024,1408]{1,0:T(8,128)} fusion(bf16[2048,1408]{1,0:T(8,128)(2,1)} %all-gather.8.cloned.1.call-done, bf16[1024,2048]{1,0:T(8,128)(2,1)} %get-tuple-element.218, f32[2048]{0:T(1024)S(1)} %convert_element_type.172, f32[1024]{0:T(1024)S(1)} %add_rsqrt_fusion.1), kind=kOutput, calls=%fused_computation.81 | convolution fusion | flops 5913968640 | bytes 15740928 | tf_op jit(solution)/shard_map/dot_general | solution.py:201
  331.8 48.5 %all-gather.10.cloned.1.call-done = bf16[2048,1408]{1,0:T(8,128)(2,1)} async-done(((bf16[128,1408]{1,0:T(8,128)(2,1)}), bf16[2048,1408]{1,0:T(8,128)(2,1)}) %all-gather.10.cloned.1.call-update) | async-done | bytes 5767184 | tf_op jit(solution)/shard_map/all_gather | solution.py:204
  380.3 65.9 %all-gather.12.cloned.1.call-done = bf16[1408,2048]{1,0:T(8,128)(2,1)} async-done(((bf16[1408,128]{1,0:T(8,128)(2,1)}), bf16[1408,2048]{1,0:T(8,128)(2,1)}) %all-gather.12.cloned.1.call-update) | async-done | bytes 5767184 | tf_op jit(solution)/shard_map/all_gather | solution.py:208
  446.2 20.9 %convolution_convert_fusion = bf16[1024,2048]{1,0:T(8,128)(2,1)} fusion(bf16[1408,2048]{1,0:T(8,128)(2,1)} %all-gather.12.cloned.1.call-done, f32[1024,1408]{1,0:T(8,128)} %fusion.47, bf16[2048,1408]{1,0:T(8,128)(2,1)} %all-gather.10.cloned.1.call-done, bf16[1024,2048]{1,0:T(8,128)(2,1)} %get-tuple-element.218, f32[2048]{0:T(1024)S(1)} %convert_element_type.172, ...), kind=kOutput, calls=%fused_computation.68 | convolution fusion | flops 11830296576 | bytes 25702400 | tf_op jit(solution)/shard_map/dot_general | solution.py:206
  469.0 5.4 %add_convert_fusion = bf16[16,1,256,512]{3,2,1,0:T(8,128)(2,1)} fusion(f32[16,1,256,512]{3,2,1,0:T(8,128)} %get-tuple-element.99, f32[256,512]{1,0:T(8,128)S(1)} %bitcast.156, f32[16,256]{1,0:T(8,128)S(1)} %bitcast_multiply_fusion.1), kind=kLoop, calls=%fused_computation.51 | loop fusion | flops 6291456 | bytes 13123584 | tf_op jit(solution)/shard_map/convert_element_type | solution.py:215
  474.3 8.4 %reduce-scatter.2.cloned.1.call-done = bf16[512,2048]{1,0:T(8,128)(2,1)} async-done(((bf16[1024,2048]{1,0:T(8,128)(2,1)}), bf16[512,2048]{1,0:T(8,128)(2,1)}) %reduce-scatter.2.cloned.1.call-update) | async-done | bytes 2097168 | tf_op jit(solution)/shard_map/reduce_scatter | solution.py:211
  482.7 4.4 add_convert_fusion.1
  (217 shorter events, 78.9 us)
Async XLA Ops:
  7.2 219.2 %copy-start = (bf16[512,2048]{1,0:T(8,128)(2,1)S(1)}, bf16[512,2048]{1,0:T(8,128)(2,1)}, u32[]{:S(2)}) copy-start(bf16[512,2048]{1,0:T(8,128)(2,1)} %param.29) | copy-start | bytes 6291460
  7.2 3.3 copy-start.7
  7.2 207.1 %all-gather.14.cloned.1.call-start = ((), (), s32[]{:S(2)}) async-start(), calls=%async_computation.5 | async-start | bytes 1310720 | tf_op jit(solution)/shard_map/all_gather | solution.py:24
  7.2 3.6 copy-start.2
  18.0 4.6 copy-start.5
  18.0 7.8 %copy-start.9 = (s32[1,16]{1,0:T(1,128)S(1)}, s32[1,16]{1,0:T(1,128)}, u32[]{:S(2)}) copy-start(s32[1,16]{1,0:T(1,128)} %param.35) | copy-start | bytes 196
  18.0 7.8 %copy-start.11 = (s32[1,16]{1,0:T(1,128)S(1)}, s32[1,16]{1,0:T(1,128)}, u32[]{:S(2)}) copy-start(s32[1,16]{1,0:T(1,128)} %param.34) | copy-start | bytes 196
  18.0 7.9 %copy-start.6 = (bf16[4,1024]{1,0:T(4,128)(2,1)S(1)}, bf16[4,1024]{1,0:T(4,128)(2,1)}, u32[]{:S(2)}) copy-start(bf16[4,1024]{1,0:T(4,128)(2,1)} %param.23) | copy-start | bytes 24580
  18.1 7.9 %copy-start.12 = (bf16[2048,16]{0,1:T(8,128)(2,1)S(1)}, bf16[2048,16]{0,1:T(8,128)(2,1)}, u32[]{:S(2)}) copy-start(bf16[2048,16]{0,1:T(8,128)(2,1)} %param.24) | copy-start | bytes 196612
  18.1 7.9 %copy-start.13 = (bf16[16,256]{1,0:T(8,128)(2,1)S(1)}, bf16[16,256]{1,0:T(8,128)(2,1)}, u32[]{:S(2)}) copy-start(bf16[16,256]{1,0:T(8,128)(2,1)} %param.25) | copy-start | bytes 24580
  18.1 7.9 %copy-start.14 = (f32[256]{0:T(256)S(1)}, f32[256]{0:T(256)}, u32[]{:S(2)}) copy-start(f32[256]{0:T(256)} %param.26) | copy-start | bytes 3076
  18.1 15.4 %collective-permute-start = (bf16[3,1024]{1,0:T(4,128)(2,1)S(1)}, bf16[3,1024]{1,0:T(4,128)(2,1)S(1)}, u32[]{:S(2)}, u32[]{:S(2)}) collective-permute-start(bf16[3,1024]{1,0:T(4,128)(2,1)S(1)} %slice_bitcast_fusion.2), channel_id=1, source_target_pairs={{0,2},{2,4},{4,6},{1,3},{3,5},{5,7},{8,10},{10,12},{12,14},{9,11},... | collective-permute-start | bytes 18440 | tf_op jit(solution)/shard_map/ppermute | solution.py:18
  30.9 1.0 copy-start.3
  40.9 1.6 copy-start.4
  44.6 144.7 %copy-start.10 = (bf16[512]{0:T(512)(128)(2,1)S(1)}, bf16[512]{0:T(512)(128)(2,1)}, u32[]{:S(2)}) copy-start(bf16[512]{0:T(512)(128)(2,1)} %param.28) | copy-start | bytes 3076
  188.6 69.4 %all-gather.16.cloned.1.call-start = ((), (), s32[]{:S(2)}) async-start(), calls=%async_computation.6 | async-start | bytes 12582912 | tf_op jit(solution)/shard_map/all_gather | solution.py:193
  230.7 2.0 copy-start.8
  230.8 89.1 %all-gather.8.cloned.1.call-start = ((), (), s32[]{:S(2)}) async-start(), calls=%async_computation.1 | async-start | bytes 6127616 | tf_op jit(solution)/shard_map/all_gather | solution.py:203
  231.5 148.8 %all-gather.10.cloned.1.call-start = ((), (), s32[]{:S(2)}) async-start(), calls=%async_computation.2 | async-start | bytes 6127616 | tf_op jit(solution)/shard_map/all_gather | solution.py:204
  232.1 214.2 %all-gather.12.cloned.1.call-start = ((), (), s32[]{:S(2)}) async-start(), calls=%async_computation.3 | async-start | bytes 6127616 | tf_op jit(solution)/shard_map/all_gather | solution.py:208
  232.7 250.1 %reduce-scatter.2.cloned.1.call-start = ((), (), s32[]{:S(2)}) async-start(), calls=%async_computation.4 | async-start | bytes 6291456 | tf_op jit(solution)/shard_map/reduce_scatter | solution.py:211
  469.0 18.2 %copy-start.1 = (bf16[512,2048]{1,0:T(8,128)(2,1)S(1)}, bf16[512,2048]{1,0:T(8,128)(2,1)}, u32[]{:S(2)}) copy-start(bf16[512,2048]{1,0:T(8,128)(2,1)} %param.29) | copy-start | bytes 6291460
Sparse Core Ops, SparseCore 0:
  188.8 25.4 all-gather.13
  230.9 27.0 all-gather.15
  260.2 59.6 all-gather.7
  321.8 58.4 all-gather.9
  382.3 63.9 all-gather.11
  467.3 15.3 reduce-scatter.1
